TPU v7x, 32 devices: a whole 2x2x4 slice. The times are simulated.
32 devices in a mesh: grp: 2 (over x), row: 16 (over z, y, core).
Axes of the slice: x: 2, y: 2, z: 4, core: 2. Of those that a mesh axis runs over, the one named last changes fastest.
Arguments:
- coordinates: float32 [3, 65536], P(None, ('grp', 'row')), parts along dimension 1, may hold values from -0.12 to 1.12, as said below
- length_scale: float32 [65536], P(('grp', 'row')), parts along dimension 0, may hold values from 0.05 to 0.4
- probes: bfloat16 [64, 65536], P(None, ('grp', 'row')), parts along dimension 1, may hold values from -6 to 6
- near_ids: int32 [256, 16], P(('grp', 'row')), parts along dimension 0, may hold values from 0 to 127, as said below
- near_count: int32 [256], P(('grp', 'row')), parts along dimension 0, may hold values from 8 to 16
- basis_out: bfloat16 [256, 32, 256], P(('grp', 'row')), parts along dimension 0, may hold values from -1 to 1
- basis_in: bfloat16 [256, 32, 256], P(('grp', 'row')), parts along dimension 0, may hold values from -0.375 to 0.375
Outputs:
- sampled: float32 [64, 65536], P(None, ('grp', 'row')), parts along dimension 1
There are 2 independent parts, one for each index of `grp`. A program takes and returns all parts, laid end to end along the dimension named above; each array names one. Nothing has to cross between parts.
Inputs may be any that keep to these rules, and one draw needn't show every extreme that they name: `coordinates`: points of one block lie within 0.12 of a common center in every coordinate. `near_ids`: row i lists i itself first, then distinct blocks whose index differs from i by at most 8; the slots from near_count[i] on hold i again.
All inputs are finite; a program needn't handle non-finite values.
Results may differ from a plain program's by a relative error of at most 0.00055.
The roundings to bfloat16 on the way count: a program that leaves them out, or rounds other values in their place, can miss the bound.
Values may be sent and summed in bfloat16 or wider, within the bound.
A program may use at most 64 MiB of HBM per device.

v0:
```python
import functools
import math

import jax
import jax.numpy as jnp
from jax import lax
from jax.experimental import pallas as pl
from jax.experimental.pallas import tpu as pltpu
from jax.sharding import PartitionSpec as P

HALO = 8
ROWS = 16
CHUNKS = 1
LOG2E = 1.0 / math.log(2.0)
C_SCALE = math.log(2.0) ** (-2.0 / 3.0)
D_SCALE = 3.0 * LOG2E * LOG2E * C_SCALE
F32 = jnp.float32
BF16 = jnp.bfloat16


def split3(x):
    high = x.astype(BF16)
    rest = x - high.astype(F32)
    mid = rest.astype(BF16)
    low = (rest - mid.astype(F32)).astype(BF16)
    return high, mid, low


def left_stack(x):
    h, m, l = [part.astype(F32) for part in split3(x)]
    return jnp.concatenate([h, h, m, h, l, m, m, l], axis=0)


def right_stack(x):
    h, m, l = split3(x)
    return jnp.concatenate([h, m, h, l, h, m, l, m], axis=0)


def matern(first, second):
    sq_dist = (first[0] - second[0]) * (first[0] - second[0])
    sq_dist = sq_dist + (first[1] - second[1]) * (first[1] - second[1])
    sq_dist = sq_dist + (first[2] - second[2]) * (first[2] - second[2])
    mean_sq = 0.5 * (first[3] * first[3] + second[3] * second[3])
    ratio = first[3] * second[3] / mean_sq
    prefac = ratio * jnp.sqrt(ratio)
    scaled = jnp.sqrt(3.0 * (sq_dist / mean_sq))
    return prefac * (1.0 + scaled) * jnp.exp(-scaled)


def nt(a, b):
    return lax.dot_general(a, b, (((1,), (1,)), ((), ())), preferred_element_type=F32)


def tn(a, b):
    return lax.dot_general(a, b, (((0,), (0,)), ((), ())), preferred_element_type=F32)


def nn(a, b):
    return lax.dot_general(a, b, (((1,), (0,)), ((), ())), preferred_element_type=F32)


def kernel(
    n, ob, bs,
    xyz_in, len_in, probes_in, ids_in, bout_in, bin_in, out_ref,
    xyz_ref, len_ref, probes_ref, ids_ref, bout_ref, bin_ref,
    xyz_r, len_r, probes_r, ids_r,
    rec_i, rec_j, cen_i, cen_j, lhs, rhs_c, mask_a, mask_b, acc, part,
    fold_all, cen_all,
    value_buf, load_sem, halo_send, halo_recv, part_send, part_recv, gat_send, gat_recv, cen_send, cen_recv,
):
    me = lax.axis_index("row")
    left = lax.rem(me + n - 1, n)
    right = lax.rem(me + 1, n)
    half = bin_ref.shape[1] // 2
    loads = [
        pltpu.make_async_copy(src, dst, load_sem.at[k])
        for k, (src, dst) in enumerate(
            (
                (xyz_in, xyz_ref), (len_in, len_ref), (ids_in, ids_ref),
                (probes_in, probes_ref), (bin_in, bin_ref), (bout_in, bout_ref),
            )
        )
    ]
    for load in loads:
        load.start()
    np_ = probes_ref.shape[0]
    width = n * ob

    barrier = pltpu.get_barrier_semaphore()

    def greet(k, carry):
        pl.semaphore_signal(barrier, inc=1, device_id={"row": lax.rem(me + k, n)})
        return carry

    lax.fori_loop(1, n, greet, 0)
    pl.semaphore_wait(barrier, n - 1)

    halo = [
        pltpu.make_async_remote_copy(
            src_ref=src, dst_ref=dst, send_sem=halo_send.at[k], recv_sem=halo_recv.at[k], device_id={"row": left}
        )
        for k, (src, dst) in enumerate(
            ((xyz_in, xyz_r), (len_in, len_r), (ids_in, ids_r), (probes_in, probes_r))
        )
    ]
    for copy in halo:
        copy.start()

    for load in loads[:5]:
        load.wait()
    row = lax.broadcasted_iota(jnp.int32, (ROWS, bs), 0)

    def fill_j(xyz, length, base):
        rec_j[0:3, base : base + ob * bs] = xyz[...]
        rec_j[3:6, base : base + ob * bs] = jnp.ones((3, ob * bs), F32)
        rec_j[6:9, base : base + ob * bs] = xyz[...]
        rec_j[9:10, base : base + ob * bs] = jnp.ones((1, ob * bs), F32)
        ln = length[...]
        rec_j[10:11, base : base + ob * bs] = ln * ln
        rec_j[11:12, base : base + ob * bs] = 1.0 / ln
        rec_j[12:16, base : base + ob * bs] = jnp.zeros((4, ob * bs), F32)
        for b in range(ob):
            at = base + b * bs
            blk = rec_j[:, at : at + bs]
            inv = rec_j[11:12, at : at + bs]
            feat = jnp.where((row == 9) | (row == 10), blk, 0.0) * (inv * (0.5 * C_SCALE))
            rhs_c[base // bs + b] = right_stack(feat)

    rec_i[0:3, :] = xyz_ref[...]
    rec_i[3:6, :] = xyz_ref[...]
    rec_i[6:9, :] = jnp.ones((3, ob * bs), F32)
    ln0 = len_ref[...]
    rec_i[9:10, :] = ln0 * ln0
    rec_i[10:11, :] = jnp.ones((1, ob * bs), F32)
    rec_i[11:12, :] = ln0
    rec_i[12:16, :] = jnp.zeros((4, ob * bs), F32)
    fill_j(xyz_ref, len_ref, 0)

    lane = lax.broadcasted_iota(jnp.int32, (ROWS, 128), 1)
    own_centers = jnp.zeros((ROWS, 128), F32)
    for b in range(ob):
        blk = rec_i[:, b * bs : (b + 1) * bs]
        mean = jnp.sum(blk, axis=1, keepdims=True) * (1.0 / bs)
        own_centers = jnp.where(lane == b, mean, own_centers)
        mean_w = jnp.broadcast_to(mean, (ROWS, bs))
        cen = jnp.where(row < 6, mean_w, 0.0)
        v = blk - cen
        feat = jnp.where((row >= 3) & (row < 6), v * v, jnp.where(row < 11, v, 0.0)) * (1.0 / rec_i[11:12, b * bs : (b + 1) * bs])
        lhs[b] = left_stack(feat).T.astype(BF16)
        mean_j = jnp.sum(rec_j[:, b * bs : (b + 1) * bs], axis=1, keepdims=True) * (1.0 / bs)
        cen_j[b] = jnp.where((row < 3) | ((row >= 6) & (row < 9)), jnp.broadcast_to(mean_j, (ROWS, bs)), 0.0)
        pb = probes_ref[:, b * bs : (b + 1) * bs]
        fold = jnp.concatenate([nt(bin_ref[b, 0:half, :], pb), nt(bin_ref[b, half:, :], pb)], axis=1)
        fold_all[me, b * half : (b + 1) * half, :] = fold.astype(BF16)
    square = jnp.concatenate([own_centers, jnp.zeros((128 - ROWS, 128), F32)], axis=0).T
    own_cols = square[0:ob, :]
    cen_all[me] = own_cols

    def gather_copies(k):
        peer = lax.rem(me + k, n)
        return (
            pltpu.make_async_remote_copy(
                src_ref=fold_all.at[me], dst_ref=fold_all.at[me],
                send_sem=gat_send.at[k], recv_sem=gat_recv.at[k], device_id={"row": peer},
            ),
            pltpu.make_async_remote_copy(
                src_ref=cen_all.at[me], dst_ref=cen_all.at[me],
                send_sem=cen_send.at[k], recv_sem=cen_recv.at[k], device_id={"row": peer},
            ),
        )

    def gather_start(k, carry):
        for copy in gather_copies(k):
            copy.start()
        return carry

    lax.fori_loop(1, n, gather_start, 0)

    acc[...] = jnp.zeros_like(acc)

    def member(ids, target):
        return jnp.max(jnp.where(ids == target, 1.0, 0.0), axis=1, keepdims=True)

    def store_rows(ref, base, value):
        wide = jnp.broadcast_to(value, (ob, bs))
        for b in range(ob):
            ref[base + b] = wide[b : b + 1, :]

    ids = ids_ref[...]
    gid = lax.broadcasted_iota(jnp.int32, ids.shape, 0) + me * ob
    for dj in range(HALO + 1):
        store_rows(mask_a, dj * ob, member(ids, gid + dj))
        if dj:
            store_rows(mask_b, dj * 2 * ob, member(ids, gid - dj))
        else:
            store_rows(mask_b, 0, jnp.zeros((ob, 1), F32))

    rows = bs // CHUNKS

    def right_side(i, jw):
        at = pl.multiple_of(jw * bs, bs)
        v = rec_j[:, pl.ds(at, bs)] - cen_j[i]
        feat = jnp.where(
            row < 3, (-2.0 * D_SCALE) * v,
            jnp.where(row < 6, D_SCALE, jnp.where(row < 9, D_SCALE * v * v, 0.0)),
        ) * rec_j[11:12, pl.ds(at, bs)]
        return jnp.concatenate([right_stack(feat), rhs_c[jw]], axis=1)

    def entries(i, side, c):
        return nn(lhs[i, c * rows : (c + 1) * rows, :], side)

    def values(both):
        w = lax.rsqrt(both[:, bs:])
        w2 = w * w
        u = jnp.maximum(both[:, :bs] * w2, 1e-30)
        s = u * lax.rsqrt(u)
        return (((w2 * w) * (LOG2E + s)) * jnp.exp2(-s)).astype(BF16)

    def products(i, jw, p_ref, p_base, slot):
        dj = jw - i
        value = value_buf[slot]
        p_j = p_ref[:, pl.ds(pl.multiple_of(p_base * bs, bs), bs)]
        p_i = probes_ref[:, pl.ds(pl.multiple_of(i * bs, bs), bs)]
        acc[i] += mask_a[dj * ob + i] * nt(p_j, value)
        acc[jw] += mask_b[dj * 2 * ob + jw] * nn(p_i, value)

    def sweep(pairs, p_ref):
        side = right_side(pairs[0][0], pairs[0][1])
        current = [entries(pairs[0][0], side, c) for c in range(CHUNKS)]
        for t, (i, jw, p_base) in enumerate(pairs):
            upcoming = None
            if t + 1 < len(pairs):
                upcoming = right_side(pairs[t + 1][0], pairs[t + 1][1])
            following = []
            for c in range(CHUNKS):
                if upcoming is not None:
                    following.append(entries(pairs[t + 1][0], upcoming, c))
                value_buf[t % 2, c * rows : (c + 1) * rows, :] = values(current[c])
                if c == 0 and t:
                    products(*pairs[t - 1][:2], p_ref, pairs[t - 1][2], (t - 1) % 2)
            current = following
        last = len(pairs) - 1
        products(*pairs[last][:2], p_ref, pairs[last][2], last % 2)

    def triangle(g, s):
        c = (s + g) // ob
        a = g + c * (ob - 1 - 2 * g)
        return a, a + s - c * (ob - g)

    def own_group(g, carry):
        pairs = []
        for s in range(ob + 1):
            i, j = triangle(g, s)
            pairs.append((i, j, j))
        sweep(pairs, probes_ref)
        return carry

    lax.fori_loop(0, ob // 4, own_group, 0)

    for copy in halo:
        copy.wait()
    fill_j(xyz_r, len_r, ob * bs)
    ids2 = ids_r[...]
    for dj in range(1, HALO + 1):
        store_rows(mask_b, dj * 2 * ob + ob, member(ids2, gid + ob - dj))

    def part_copy(col):
        return pltpu.make_async_remote_copy(
            src_ref=acc.at[ob + col], dst_ref=part.at[col],
            send_sem=part_send.at[col], recv_sem=part_recv.at[col], device_id={"row": right},
        )

    def cross_group(g, carry):
        pairs = []
        for s in range(ob + 1):
            col, i = triangle(g, s)
            pairs.append((i, ob + col, col))
        sweep(pairs, probes_r)
        part_copy(g).start()
        part_copy(ob - 1 - g).start()
        return carry

    lax.fori_loop(0, ob // 2, cross_group, 0)
    lax.fori_loop(ob // 4, ob // 2, own_group, 0)

    def gather_wait(k, carry):
        for copy in gather_copies(k):
            copy.wait()
        return carry

    lax.fori_loop(1, n, gather_wait, 0)
    centers = cen_all[...].reshape(width, 128).T
    picks = (0, 1, 2, 11)
    coupling = matern([own_cols[:, c : c + 1] for c in picks], [centers[c : c + 1, :] for c in picks])
    global_ids = lax.broadcasted_iota(jnp.int32, (ob, width), 1)
    near = jnp.zeros((ob, width), F32)
    for t in range(ids.shape[1]):
        near = jnp.where(ids[:, t : t + 1] == global_ids, 1.0, near)
    coupling = jnp.where(near > 0.0, 0.0, coupling).astype(BF16)

    step_w = 128
    total = jnp.zeros((ob * half, 2 * np_), F32)
    pick_r = lax.broadcasted_iota(jnp.int32, (step_w, step_w * half), 0)
    pick_c = lax.broadcasted_iota(jnp.int32, (step_w, step_w * half), 1)
    spread = jnp.where(pick_c // half == pick_r, 1.0, 0.0).astype(BF16)
    eye_r = lax.broadcasted_iota(jnp.int32, (ob * half, step_w * half), 0)
    eye_c = lax.broadcasted_iota(jnp.int32, (ob * half, step_w * half), 1)
    same = lax.rem(eye_r, half) == lax.rem(eye_c, half)
    per = step_w // ob
    for q in range(width // step_w):
        wide = nn(coupling[:, q * step_w : (q + 1) * step_w], spread)
        wide = jnp.concatenate(
            [jnp.broadcast_to(wide[i : i + 1, :], (half, step_w * half)) for i in range(ob)], axis=0
        )
        kron = jnp.where(same, wide, 0.0).astype(BF16)
        folded = fold_all[q * per : (q + 1) * per].reshape(step_w * half, 2 * np_)
        total = total + nn(kron, folded)
    summed = total.astype(BF16)

    loads[5].wait()
    for b in range(ob):
        part_copy(b).wait()
    for b in range(ob):
        mine = summed[b * half : (b + 1) * half, :]
        far = tn(mine[:, :np_], bout_ref[b, 0:half, :]) + tn(mine[:, np_:], bout_ref[b, half:, :])
        out_ref[:, b * bs : (b + 1) * bs] = acc[b] + part[b] + far


def solution(mesh):
    n = mesh.shape["row"]

    def shards(coordinates, length_scale, probes, near_ids, near_count, basis_out, basis_in):
        ob, rank, bs = basis_out.shape
        np_ = probes.shape[0]
        own = ob * bs
        slots = near_ids.shape[1]
        vmem = pl.BlockSpec(memory_space=pltpu.VMEM)
        dma = pltpu.SemaphoreType.DMA
        return pl.pallas_call(
            functools.partial(kernel, n, ob, bs),
            out_shape=jax.ShapeDtypeStruct((np_, own), F32),
            in_specs=[pl.BlockSpec(memory_space=pl.ANY)] * 6,
            out_specs=vmem,
            scratch_shapes=[
                pltpu.VMEM((3, own), F32),
                pltpu.VMEM((1, own), F32),
                pltpu.VMEM((np_, own), BF16),
                pltpu.VMEM((ob, slots), jnp.int32),
                pltpu.VMEM((ob, rank, bs), BF16),
                pltpu.VMEM((ob, rank, bs), BF16),
                pltpu.VMEM((3, own), F32),
                pltpu.VMEM((1, own), F32),
                pltpu.VMEM((np_, own), BF16),
                pltpu.VMEM((ob, slots), jnp.int32),
                pltpu.VMEM((ROWS, own), F32),
                pltpu.VMEM((ROWS, 2 * own), F32),
                pltpu.VMEM((ob, ROWS, bs), F32),
                pltpu.VMEM((ob, ROWS, bs), F32),
                pltpu.VMEM((ob, bs, 8 * ROWS), BF16),
                pltpu.VMEM((2 * ob, 8 * ROWS, bs), BF16),
                pltpu.VMEM(((HALO + 1) * ob, 1, bs), F32),
                pltpu.VMEM(((HALO + 1) * 2 * ob, 1, bs), F32),
                pltpu.VMEM((2 * ob, np_, bs), F32),
                pltpu.VMEM((ob, np_, bs), F32),
                pltpu.VMEM((n, ob * rank // 2, 2 * np_), BF16),
                pltpu.VMEM((n, ob, 128), F32),
                pltpu.VMEM((2, bs, bs), BF16),
                dma((6,)), dma((4,)), dma((4,)), dma((ob,)), dma((ob,)),
                dma((n,)), dma((n,)), dma((n,)), dma((n,)),
            ],
            compiler_params=pltpu.CompilerParams(collective_id=0, has_side_effects=True, vmem_limit_bytes=60 * 1024 * 1024),
        )(coordinates, length_scale.reshape(1, own), probes, near_ids, basis_out, basis_in)

    placed = (
        P(None, ("grp", "row")),
        P(("grp", "row")),
        P(None, ("grp", "row")),
        P(("grp", "row"), None),
        P(("grp", "row")),
        P(("grp", "row"), None, None),
        P(("grp", "row"), None, None),
    )
    return jax.shard_map(
        shards, mesh=mesh, in_specs=placed, out_specs=P(None, ("grp", "row")), check_vma=False
    )
```

profile of v0, /device:TPU:15, one launch (start us, length us, event | category | flops | bytes accessed | tf_op | source)
XLA Modules:
  0.0 33.4 jit_solution(8918103069060240411)
XLA Ops:
  0.0 31.5 %shard_map.64 = f32[64,2048]{1,0:T(8,128)} custom-call(f32[3,2048]{1,0:T(4,128)} %xyz_in.1, f32[1,2048]{1,0:T(1,128)} %bitcast.1, bf16[64,2048]{1,0:T(8,128)(2,1)} %probes_in.1, s32[8,16]{1,0:T(8,128)} %ids_in.1, bf16[8,32,256]{2,1,0:T(8,128)(2,1)} %bout_in.1, bf16[8,32,256]{2,1,0:T(8,128)(2,1)} %bin_in.1), custom_call_target="tpu_custom_call" | custom-call | tf_op jit(solution)/shard_map/pallas_call | solution.py:339
  31.5 1.9 %copy.8 = f32[64,2048]{1,0:T(8,128)} copy(f32[64,2048]{1,0:T(8,128)} %shard_map.64) | data formatting | bytes 1048576
where the time goes:
time: 33.6 us; the launch traced here: 33.4 us
  Pallas kernels  31.5 us (94%)
  local copies, waits for them, and re-layouts  1.87 us (6%)
    pallas_call x1, Pallas kernels, shards(): pl.pallas_call(functools.partial(kernel, n, ob, bs), out_shape=jax.ShapeD...  31.5 us
    unnamed x1, local copies, waits for them, and re-layouts  1.87 us

commit v1 on v0

--- a/solution.py
+++ b/solution.py
@@ -11,6 +11,8 @@
 HALO = 8
 ROWS = 16
 CHUNKS = 1
+OWN_FIRST = 3
+OPEN_AT = 1
 LOG2E = 1.0 / math.log(2.0)
 C_SCALE = math.log(2.0) ** (-2.0 / 3.0)
 D_SCALE = 3.0 * LOG2E * LOG2E * C_SCALE
@@ -59,52 +61,100 @@
     return lax.dot_general(a, b, (((1,), (0,)), ((), ())), preferred_element_type=F32)
 
 
+def bit_reverse(x, bits):
+    out = x * 0
+    for k in range(bits):
+        out = out + (x // 2 ** k) % 2 * 2 ** (bits - 1 - k)
+    return out
+
+
 def kernel(
     n, ob, bs,
     xyz_in, len_in, probes_in, ids_in, bout_in, bin_in, out_ref,
     xyz_ref, len_ref, probes_ref, ids_ref, bout_ref, bin_ref,
-    xyz_r, len_r, probes_r, ids_r,
-    rec_i, rec_j, cen_i, cen_j, lhs, rhs_c, mask_a, mask_b, acc, part,
+    xyz_r, len_r, ids_r,
+    rec_i, rec_j, cen_j, lhs, rhs_c, mask_a, mask_b, acc, part,
     fold_all, cen_all,
     value_buf, load_sem, halo_send, halo_recv, part_send, part_recv, gat_send, gat_recv, cen_send, cen_recv,
 ):
     me = lax.axis_index("row")
-    left = lax.rem(me + n - 1, n)
-    right = lax.rem(me + 1, n)
+    bits = n.bit_length() - 1
+    own = ob * bs
+    left = jnp.maximum(me - 1, 0)
+    right = jnp.minimum(me + 1, n - 1)
+    has_left = me > 0
+    has_right = me < n - 1
+    place = bit_reverse(me, bits)
     half = bin_ref.shape[1] // 2
+    np_ = probes_ref.shape[0]
+    width = n * ob
+    own_probes = probes_ref.at[:, 0:own]
     loads = [
         pltpu.make_async_copy(src, dst, load_sem.at[k])
         for k, (src, dst) in enumerate(
             (
                 (xyz_in, xyz_ref), (len_in, len_ref), (ids_in, ids_ref),
-                (probes_in, probes_ref), (bin_in, bin_ref), (bout_in, bout_ref),
+                (probes_in, own_probes), (bin_in, bin_ref), (bout_in, bout_ref),
             )
         )
     ]
     for load in loads:
         load.start()
-    np_ = probes_ref.shape[0]
-    width = n * ob
+
+    def partner(step):
+        bit = 2 ** (bits - 1 - step)
+        return me + bit * (1 - 2 * (me // bit % 2))
 
     barrier = pltpu.get_barrier_semaphore()
 
-    def greet(k, carry):
-        pl.semaphore_signal(barrier, inc=1, device_id={"row": lax.rem(me + k, n)})
-        return carry
-
-    lax.fori_loop(1, n, greet, 0)
-    pl.semaphore_wait(barrier, n - 1)
+    @pl.when(has_left)
+    def _():
+        pl.semaphore_signal(barrier, inc=1, device_id={"row": left})
+
+    @pl.when(has_right)
+    def _():
+        pl.semaphore_signal(barrier, inc=1, device_id={"row": right})
+
+    for step in range(bits):
+        pl.semaphore_signal(barrier, inc=1, device_id={"row": partner(step)})
 
     halo = [
         pltpu.make_async_remote_copy(
             src_ref=src, dst_ref=dst, send_sem=halo_send.at[k], recv_sem=halo_recv.at[k], device_id={"row": left}
         )
         for k, (src, dst) in enumerate(
-            ((xyz_in, xyz_r), (len_in, len_r), (ids_in, ids_r), (probes_in, probes_r))
+            ((xyz_in, xyz_r), (len_in, len_r), (ids_in, ids_r), (probes_in, probes_ref.at[:, own:]))
         )
     ]
-    for copy in halo:
-        copy.start()
+
+    def gather_copies(step):
+        size = 2 ** step
+        held = pl.ds(place // size * size, size)
+        peer = {"row": partner(step)}
+        return (
+            pltpu.make_async_remote_copy(
+                src_ref=fold_all.at[held], dst_ref=fold_all.at[held],
+                send_sem=gat_send.at[step], recv_sem=gat_recv.at[step], device_id=peer,
+            ),
+            pltpu.make_async_remote_copy(
+                src_ref=cen_all.at[held], dst_ref=cen_all.at[held],
+                send_sem=cen_send.at[step], recv_sem=cen_recv.at[step], device_id=peer,
+            ),
+        )
+
+    def gather_start(step):
+        for copy in gather_copies(step):
+            copy.start()
+
+    def gather_wait(step):
+        for copy in gather_copies(step):
+            copy.wait()
+
+    def part_copy(col):
+        return pltpu.make_async_remote_copy(
+            src_ref=acc.at[ob + col], dst_ref=part.at[col],
+            send_sem=part_send.at[col], recv_sem=part_recv.at[col], device_id={"row": right},
+        )
 
     for load in loads[:5]:
         load.wait()
@@ -151,30 +201,10 @@
         cen_j[b] = jnp.where((row < 3) | ((row >= 6) & (row < 9)), jnp.broadcast_to(mean_j, (ROWS, bs)), 0.0)
         pb = probes_ref[:, b * bs : (b + 1) * bs]
         fold = jnp.concatenate([nt(bin_ref[b, 0:half, :], pb), nt(bin_ref[b, half:, :], pb)], axis=1)
-        fold_all[me, b * half : (b + 1) * half, :] = fold.astype(BF16)
+        fold_all[place, b * half : (b + 1) * half, :] = fold.astype(BF16)
     square = jnp.concatenate([own_centers, jnp.zeros((128 - ROWS, 128), F32)], axis=0).T
     own_cols = square[0:ob, :]
-    cen_all[me] = own_cols
-
-    def gather_copies(k):
-        peer = lax.rem(me + k, n)
-        return (
-            pltpu.make_async_remote_copy(
-                src_ref=fold_all.at[me], dst_ref=fold_all.at[me],
-                send_sem=gat_send.at[k], recv_sem=gat_recv.at[k], device_id={"row": peer},
-            ),
-            pltpu.make_async_remote_copy(
-                src_ref=cen_all.at[me], dst_ref=cen_all.at[me],
-                send_sem=cen_send.at[k], recv_sem=cen_recv.at[k], device_id={"row": peer},
-            ),
-        )
-
-    def gather_start(k, carry):
-        for copy in gather_copies(k):
-            copy.start()
-        return carry
-
-    lax.fori_loop(1, n, gather_start, 0)
+    cen_all[place] = own_cols
 
     acc[...] = jnp.zeros_like(acc)
 
@@ -216,83 +246,102 @@
         s = u * lax.rsqrt(u)
         return (((w2 * w) * (LOG2E + s)) * jnp.exp2(-s)).astype(BF16)
 
-    def products(i, jw, p_ref, p_base, slot):
+    def products(i, jw, slot):
         dj = jw - i
         value = value_buf[slot]
-        p_j = p_ref[:, pl.ds(pl.multiple_of(p_base * bs, bs), bs)]
+        p_j = probes_ref[:, pl.ds(pl.multiple_of(jw * bs, bs), bs)]
         p_i = probes_ref[:, pl.ds(pl.multiple_of(i * bs, bs), bs)]
         acc[i] += mask_a[dj * ob + i] * nt(p_j, value)
         acc[jw] += mask_b[dj * 2 * ob + jw] * nn(p_i, value)
 
-    def sweep(pairs, p_ref):
-        side = right_side(pairs[0][0], pairs[0][1])
+    def sweep(pairs):
+        side = right_side(*pairs[0])
         current = [entries(pairs[0][0], side, c) for c in range(CHUNKS)]
-        for t, (i, jw, p_base) in enumerate(pairs):
+        for t, (i, jw) in enumerate(pairs):
             upcoming = None
             if t + 1 < len(pairs):
-                upcoming = right_side(pairs[t + 1][0], pairs[t + 1][1])
+                upcoming = right_side(*pairs[t + 1])
             following = []
             for c in range(CHUNKS):
                 if upcoming is not None:
                     following.append(entries(pairs[t + 1][0], upcoming, c))
                 value_buf[t % 2, c * rows : (c + 1) * rows, :] = values(current[c])
                 if c == 0 and t:
-                    products(*pairs[t - 1][:2], p_ref, pairs[t - 1][2], (t - 1) % 2)
+                    products(*pairs[t - 1], (t - 1) % 2)
             current = following
         last = len(pairs) - 1
-        products(*pairs[last][:2], p_ref, pairs[last][2], last % 2)
+        products(*pairs[last], last % 2)
 
     def triangle(g, s):
         c = (s + g) // ob
         a = g + c * (ob - 1 - 2 * g)
         return a, a + s - c * (ob - g)
 
-    def own_group(g, carry):
+    groups = ob // 2
+    ahead = min(OWN_FIRST, groups)
+
+    def open_links():
+        pl.semaphore_wait(barrier, bits + jnp.where(has_left, 1, 0) + jnp.where(has_right, 1, 0))
+
+        @pl.when(has_left)
+        def _():
+            for copy in halo:
+                copy.start()
+
+        gather_start(0)
+
+    def take_halo():
+        @pl.when(has_right)
+        def _():
+            for copy in halo:
+                copy.wait_recv()
+
+        @pl.when(jnp.logical_not(has_right))
+        def _():
+            xyz_r[...] = xyz_ref[...]
+            len_r[...] = len_ref[...]
+            ids_r[...] = ids_ref[...]
+            probes_ref[:, own:] = probes_ref[:, 0:own]
+
+        fill_j(xyz_r, len_r, own)
+        ids2 = ids_r[...]
+        for dj in range(1, HALO + 1):
+            store_rows(mask_b, dj * 2 * ob + ob, member(ids2, gid + ob - dj))
+
+    def advance(step):
+        gather_wait(step - 1)
+        gather_start(step)
+
+    hooks = [(OPEN_AT, open_links), (ahead, take_halo)]
+    for step in range(1, bits):
+        hooks.append((min(OPEN_AT + 1 + step, 2 * groups - 1), functools.partial(advance, step)))
+
+    def group(t, carry):
+        for at, hook in hooks:
+            pl.when(t == at)(hook)
+        cross = jnp.logical_and(t >= ahead, t < ahead + groups)
+        g = t - jnp.where(t < ahead, 0, jnp.where(cross, ahead, groups))
         pairs = []
         for s in range(ob + 1):
-            i, j = triangle(g, s)
-            pairs.append((i, j, j))
-        sweep(pairs, probes_ref)
+            a, b = triangle(g, s)
+            pairs.append((jnp.where(cross, b, a), jnp.where(cross, ob + a, b)))
+        sweep(pairs)
+
+        @pl.when(jnp.logical_and(cross, has_right))
+        def _():
+            part_copy(g).start()
+            part_copy(ob - 1 - g).start()
+
         return carry
 
-    lax.fori_loop(0, ob // 4, own_group, 0)
-
-    for copy in halo:
-        copy.wait()
-    fill_j(xyz_r, len_r, ob * bs)
-    ids2 = ids_r[...]
-    for dj in range(1, HALO + 1):
-        store_rows(mask_b, dj * 2 * ob + ob, member(ids2, gid + ob - dj))
-
-    def part_copy(col):
-        return pltpu.make_async_remote_copy(
-            src_ref=acc.at[ob + col], dst_ref=part.at[col],
-            send_sem=part_send.at[col], recv_sem=part_recv.at[col], device_id={"row": right},
-        )
-
-    def cross_group(g, carry):
-        pairs = []
-        for s in range(ob + 1):
-            col, i = triangle(g, s)
-            pairs.append((i, ob + col, col))
-        sweep(pairs, probes_r)
-        part_copy(g).start()
-        part_copy(ob - 1 - g).start()
-        return carry
-
-    lax.fori_loop(0, ob // 2, cross_group, 0)
-    lax.fori_loop(ob // 4, ob // 2, own_group, 0)
-
-    def gather_wait(k, carry):
-        for copy in gather_copies(k):
-            copy.wait()
-        return carry
-
-    lax.fori_loop(1, n, gather_wait, 0)
+    lax.fori_loop(0, 2 * groups, group, 0)
+
+    gather_wait(bits - 1)
     centers = cen_all[...].reshape(width, 128).T
     picks = (0, 1, 2, 11)
     coupling = matern([own_cols[:, c : c + 1] for c in picks], [centers[c : c + 1, :] for c in picks])
-    global_ids = lax.broadcasted_iota(jnp.int32, (ob, width), 1)
+    column = lax.broadcasted_iota(jnp.int32, (ob, width), 1)
+    global_ids = bit_reverse(column // ob, bits) * ob + column % ob
     near = jnp.zeros((ob, width), F32)
     for t in range(ids.shape[1]):
         near = jnp.where(ids[:, t : t + 1] == global_ids, 1.0, near)
@@ -318,12 +367,27 @@
     summed = total.astype(BF16)
 
     loads[5].wait()
-    for b in range(ob):
-        part_copy(b).wait()
+
+    @pl.when(has_left)
+    def _():
+        for copy in halo:
+            copy.wait_send()
+        for b in range(ob):
+            part_copy(b).wait_recv()
+
+    @pl.when(jnp.logical_not(has_left))
+    def _():
+        part[...] = jnp.zeros_like(part)
+
     for b in range(ob):
         mine = summed[b * half : (b + 1) * half, :]
         far = tn(mine[:, :np_], bout_ref[b, 0:half, :]) + tn(mine[:, np_:], bout_ref[b, half:, :])
         out_ref[:, b * bs : (b + 1) * bs] = acc[b] + part[b] + far
+
+    @pl.when(has_right)
+    def _():
+        for b in range(ob):
+            part_copy(b).wait_send()
 
 
 def solution(mesh):
@@ -344,17 +408,15 @@
             scratch_shapes=[
                 pltpu.VMEM((3, own), F32),
                 pltpu.VMEM((1, own), F32),
-                pltpu.VMEM((np_, own), BF16),
+                pltpu.VMEM((np_, 2 * own), BF16),
                 pltpu.VMEM((ob, slots), jnp.int32),
                 pltpu.VMEM((ob, rank, bs), BF16),
                 pltpu.VMEM((ob, rank, bs), BF16),
                 pltpu.VMEM((3, own), F32),
                 pltpu.VMEM((1, own), F32),
-                pltpu.VMEM((np_, own), BF16),
                 pltpu.VMEM((ob, slots), jnp.int32),
                 pltpu.VMEM((ROWS, own), F32),
                 pltpu.VMEM((ROWS, 2 * own), F32),
-                pltpu.VMEM((ob, ROWS, bs), F32),
                 pltpu.VMEM((ob, ROWS, bs), F32),
                 pltpu.VMEM((ob, bs, 8 * ROWS), BF16),
                 pltpu.VMEM((2 * ob, 8 * ROWS, bs), BF16),

time: 33.6 us -> 30.5 us (0.908)
  the two profiles are of different devices: /device:TPU:15 before, /device:TPU:12 now
where the time goes in v1:
time: 30.5 us; the launch traced here: 30.3 us
  Pallas kernels  28.4 us (93%)
  local copies, waits for them, and re-layouts  1.87 us (6%)
    pallas_call x1, Pallas kernels, shards(): pl.pallas_call(functools.partial(kernel, n, ob, bs), out_shape=jax.ShapeD...  28.4 us
    unnamed x1, local copies, waits for them, and re-layouts  1.87 us

profile of v1, /device:TPU:12, one launch (start us, length us, event | category | flops | bytes accessed | tf_op | source)
XLA Modules:
  0.0 30.3 jit_solution(5569441761377089685)
XLA Ops:
  0.0 28.4 %shard_map.64 = f32[64,2048]{1,0:T(8,128)} custom-call(f32[3,2048]{1,0:T(4,128)} %xyz_in.1, f32[1,2048]{1,0:T(1,128)} %bitcast.1, bf16[64,2048]{1,0:T(8,128)(2,1)} %probes_in.1, s32[8,16]{1,0:T(8,128)} %ids_in.1, bf16[8,32,256]{2,1,0:T(8,128)(2,1)} %bout_in.1, bf16[8,32,256]{2,1,0:T(8,128)(2,1)} %bin_in.1), custom_call_target="tpu_custom_call" | custom-call | tf_op jit(solution)/shard_map/pallas_call | solution.py:403
  28.4 1.9 %copy.8 = f32[64,2048]{1,0:T(8,128)} copy(f32[64,2048]{1,0:T(8,128)} %shard_map.64) | data formatting | bytes 1048576

commit v2 on v1

v2 whole, which is shorter than its diff:
```python
import functools
import math

import jax
import jax.numpy as jnp
from jax import lax
from jax.experimental import pallas as pl
from jax.experimental.pallas import tpu as pltpu
from jax.sharding import PartitionSpec as P

HALO = 8
ROWS = 16
OPEN_AT = 1
LEVEL_AT = 8
LOG2E = 1.0 / math.log(2.0)
C_SCALE = math.log(2.0) ** (-2.0 / 3.0)
D_SCALE = 3.0 * LOG2E * LOG2E * C_SCALE
F32 = jnp.float32
BF16 = jnp.bfloat16


def split3(x):
    high = x.astype(BF16)
    rest = x - high.astype(F32)
    mid = rest.astype(BF16)
    low = (rest - mid.astype(F32)).astype(BF16)
    return high, mid, low


def left_stack(x):
    h, m, l = [part.astype(F32) for part in split3(x)]
    return jnp.concatenate([h, h, m, h, l, m, m, l], axis=0)


def right_stack(x):
    h, m, l = split3(x)
    return jnp.concatenate([h, m, h, l, h, m, l, m], axis=0)


def matern(first, second):
    sq_dist = (first[0] - second[0]) * (first[0] - second[0])
    sq_dist = sq_dist + (first[1] - second[1]) * (first[1] - second[1])
    sq_dist = sq_dist + (first[2] - second[2]) * (first[2] - second[2])
    mean_sq = 0.5 * (first[3] * first[3] + second[3] * second[3])
    ratio = first[3] * second[3] / mean_sq
    prefac = ratio * jnp.sqrt(ratio)
    scaled = jnp.sqrt(3.0 * (sq_dist / mean_sq))
    return prefac * (1.0 + scaled) * jnp.exp(-scaled)


def nt(a, b):
    return lax.dot_general(a, b, (((1,), (1,)), ((), ())), preferred_element_type=F32)


def tn(a, b):
    return lax.dot_general(a, b, (((0,), (0,)), ((), ())), preferred_element_type=F32)


def nn(a, b):
    return lax.dot_general(a, b, (((1,), (0,)), ((), ())), preferred_element_type=F32)


def kernel(
    n, ob, bs,
    xyz_in, len_in, probes_in, ids_in, bout_in, bin_in, out_ref,
    xyz_ref, len_ref, ids_ref, bout_ref, bin_ref,
    xyz_h, len_h, ids_h, probes,
    rec_i, rec_j, cen_j, lhs, rhs_c, mask, acc, part,
    fold_all, cen_all, cen_y, red_out, red_in,
    value_buf, load_sem, halo_send, halo_recv, part_send, part_recv,
    gat_send, gat_recv, cen_send, cen_recv, low_send, low_recv,
):
    me = lax.axis_index("row")
    own = ob * bs
    h = ob // 2
    window = ob + 2 * h
    hb = h * bs
    quads = n // 4
    core = me % 2
    col_y = me // 2 % 2
    hi = me // 4
    fast = me + 1 - 2 * core
    slow = jnp.clip(me - 1 + 2 * core, 0, n - 1)
    has_left = me > 0
    has_right = me < n - 1
    has_slow = jnp.where(core == 0, has_left, has_right)
    across = me + 2 - 4 * col_y
    side_fast = 1 - core
    side_slow = core
    half = bin_ref.shape[1] // 2
    np_ = probes.shape[0]
    width = n // 2 * ob

    loads = [
        pltpu.make_async_copy(src, dst, load_sem.at[k])
        for k, (src, dst) in enumerate(
            (
                (xyz_in, xyz_ref), (len_in, len_ref), (ids_in, ids_ref),
                (probes_in, probes.at[:, hb : hb + own]), (bin_in, bin_ref), (bout_in, bout_ref),
            )
        )
    ]
    for load in loads:
        load.start()

    barrier = pltpu.get_barrier_semaphore()

    def greet(peer):
        pl.semaphore_signal(barrier, inc=1, device_id={"row": peer})

    greet(fast)
    pl.when(has_slow)(lambda: greet(slow))
    greet(across)

    def level(k):
        return lax.rem(hi + k, quads) * 4 + me % 4

    for k in range(1, quads):
        greet(level(k))

    def lanes(start, size):
        return pl.ds(pl.multiple_of(start, size), size)

    def halo_out(side, peer):
        src = lanes(side * hb, hb)
        there = 1 - side
        pairs = (
            (xyz_in.at[:, src], xyz_h.at[there]),
            (len_in.at[:, src], len_h.at[there]),
            (ids_in, ids_h.at[there]),
            (probes_in.at[:, src], probes.at[:, lanes(there * (own + hb), hb)]),
        )
        return [
            pltpu.make_async_remote_copy(
                src_ref=a, dst_ref=b, send_sem=halo_send.at[side, k], recv_sem=halo_recv.at[there, k],
                device_id={"row": peer},
            )
            for k, (a, b) in enumerate(pairs)
        ]

    def halo_arrival(side, peer):
        pairs = (
            (xyz_in.at[:, 0:hb], xyz_h.at[side]),
            (len_in.at[:, 0:hb], len_h.at[side]),
            (ids_in, ids_h.at[side]),
            (probes_in.at[:, 0:hb], probes.at[:, lanes(side * (own + hb), hb)]),
        )
        return [
            pltpu.make_async_remote_copy(
                src_ref=a, dst_ref=b, send_sem=halo_send.at[side, k], recv_sem=halo_recv.at[side, k],
                device_id={"row": peer},
            )
            for k, (a, b) in enumerate(pairs)
        ]

    slot = core * quads + hi

    def level_copies(k, source):
        at = core * quads + source
        return [
            pltpu.make_async_remote_copy(
                src_ref=fold_all.at[at], dst_ref=fold_all.at[at],
                send_sem=gat_send.at[k], recv_sem=gat_recv.at[k], device_id={"row": level(k)},
            ),
            pltpu.make_async_remote_copy(
                src_ref=cen_all.at[at], dst_ref=cen_all.at[at],
                send_sem=cen_send.at[k], recv_sem=cen_recv.at[k], device_id={"row": level(k)},
            ),
        ]

    def core_copies(which):
        held = pl.ds(which * quads, quads)
        return [
            pltpu.make_async_remote_copy(
                src_ref=fold_all.at[held], dst_ref=fold_all.at[held],
                send_sem=low_send.at[0], recv_sem=low_recv.at[0], device_id={"row": fast},
            ),
            pltpu.make_async_remote_copy(
                src_ref=cen_all.at[held], dst_ref=cen_all.at[held],
                send_sem=low_send.at[1], recv_sem=low_recv.at[1], device_id={"row": fast},
            ),
        ]

    center_copy = pltpu.make_async_remote_copy(
        src_ref=cen_all.at[slot], dst_ref=cen_y,
        send_sem=low_send.at[2], recv_sem=low_recv.at[2], device_id={"row": across},
    )
    sum_copy = pltpu.make_async_remote_copy(
        src_ref=red_out, dst_ref=red_in,
        send_sem=low_send.at[3], recv_sem=low_recv.at[3], device_id={"row": across},
    )

    def part_copy(side, x, peer):
        return pltpu.make_async_remote_copy(
            src_ref=acc.at[(ob + h) * side + x], dst_ref=part.at[h * (1 - side) + x],
            send_sem=part_send.at[side * h + x], recv_sem=part_recv.at[h * (1 - side) + x],
            device_id={"row": peer},
        )

    def part_arrival(b, peer):
        return pltpu.make_async_remote_copy(
            src_ref=acc.at[b], dst_ref=part.at[b],
            send_sem=part_send.at[b], recv_sem=part_recv.at[b], device_id={"row": peer},
        )

    for load in loads[:5]:
        load.wait()
    row = lax.broadcasted_iota(jnp.int32, (ROWS, bs), 0)

    def fill_j(at, xyz, ln):
        rec_j[at, 0:3, :] = xyz
        rec_j[at, 3:6, :] = jnp.ones((3, bs), F32)
        rec_j[at, 6:9, :] = xyz
        rec_j[at, 9:10, :] = jnp.ones((1, bs), F32)
        rec_j[at, 10:11, :] = ln * ln
        rec_j[at, 11:12, :] = 1.0 / ln
        rec_j[at, 12:16, :] = jnp.zeros((4, bs), F32)
        feat = jnp.where((row == 9) | (row == 10), rec_j[at], 0.0) * (rec_j[at, 11:12, :] * (0.5 * C_SCALE))
        rhs_c[at] = right_stack(feat)

    rec_i[0:3, :] = xyz_ref[...]
    rec_i[3:6, :] = xyz_ref[...]
    rec_i[6:9, :] = jnp.ones((3, own), F32)
    ln0 = len_ref[...]
    rec_i[9:10, :] = ln0 * ln0
    rec_i[10:11, :] = jnp.ones((1, own), F32)
    rec_i[11:12, :] = ln0
    rec_i[12:16, :] = jnp.zeros((4, own), F32)

    ids = ids_ref[...]
    slots = ids.shape[1]
    lane = lax.broadcasted_iota(jnp.int32, (ROWS, 128), 1)
    own_centers = jnp.zeros((ROWS, 128), F32)
    for b in range(ob):
        blk = rec_i[:, b * bs : (b + 1) * bs]
        mean = jnp.sum(blk, axis=1, keepdims=True) * (1.0 / bs)
        own_centers = jnp.where(lane == b, mean, own_centers)
        mean_w = jnp.broadcast_to(mean, (ROWS, bs))
        cen = jnp.where(row < 6, mean_w, 0.0)
        v = blk - cen
        feat = jnp.where((row >= 3) & (row < 6), v * v, jnp.where(row < 11, v, 0.0)) * (1.0 / rec_i[11:12, b * bs : (b + 1) * bs])
        lhs[b] = left_stack(feat).T.astype(BF16)
        fill_j(h + b, xyz_ref[:, b * bs : (b + 1) * bs], len_ref[:, b * bs : (b + 1) * bs])
        mean_j = jnp.sum(rec_j[h + b], axis=1, keepdims=True) * (1.0 / bs)
        cen_j[b] = jnp.where((row < 3) | ((row >= 6) & (row < 9)), jnp.broadcast_to(mean_j, (ROWS, bs)), 0.0)
        pb = probes[:, hb + b * bs : hb + (b + 1) * bs]
        fold = jnp.concatenate([nt(bin_ref[b, 0:half, :], pb), nt(bin_ref[b, half:, :], pb)], axis=1)
        fold_all[slot, b * half : (b + 1) * half, :] = fold.astype(BF16)
    square = jnp.concatenate([own_centers, jnp.zeros((128 - ROWS, 128), F32)], axis=0).T
    id_rows = jnp.concatenate(
        [jnp.zeros((ob, ROWS), F32), ids.astype(F32), jnp.zeros((ob, 128 - ROWS - slots), F32)], axis=1
    )
    own_cols = square[0:ob, :] + id_rows
    cen_all[slot] = own_cols

    acc[...] = jnp.zeros_like(acc)

    def member(ids, target):
        return jnp.max(jnp.where(ids == target, 1.0, 0.0), axis=1, keepdims=True)

    gid = lax.broadcasted_iota(jnp.int32, ids.shape, 0) + me * ob

    def mask_at(offset, q):
        return (offset + HALO) * window + q

    for offset in range(-HALO, HALO + 1):
        wide = jnp.broadcast_to(member(ids, gid + offset), (ob, bs))
        for b in range(ob):
            mask[mask_at(offset, h + b)] = wide[b : b + 1, :]
    blank = (2 * HALO + 1) * window
    mask[blank] = jnp.zeros((1, bs), F32)

    def right_side(o, q):
        v = rec_j[q] - cen_j[o]
        feat = jnp.where(
            row < 3, (-2.0 * D_SCALE) * v,
            jnp.where(row < 6, D_SCALE, jnp.where(row < 9, D_SCALE * v * v, 0.0)),
        ) * rec_j[q, 11:12, :]
        return jnp.concatenate([right_stack(feat), rhs_c[q]], axis=1)

    def values(both):
        w = lax.rsqrt(both[:, bs:])
        w2 = w * w
        u = jnp.maximum(both[:, :bs] * w2, 1e-30)
        s = u * lax.rsqrt(u)
        return (((w2 * w) * (LOG2E + s)) * jnp.exp2(-s)).astype(BF16)

    def products(o, q, turn):
        offset = q - h - o
        value = value_buf[turn]
        p_q = probes[:, lanes(q * bs, bs)]
        p_o = probes[:, lanes((h + o) * bs, bs)]
        acc[h + o] += mask[mask_at(offset, h + o)] * nt(p_q, value)
        acc[q] += mask[jnp.where(offset == 0, blank, mask_at(-offset, q))] * nn(p_o, value)

    def sweep(pairs):
        current = nn(lhs[pairs[0][0]], right_side(*pairs[0]))
        for t, pair in enumerate(pairs):
            if t + 1 < len(pairs):
                following = nn(lhs[pairs[t + 1][0]], right_side(*pairs[t + 1]))
            value_buf[t % 2] = values(current)
            if t:
                products(*pairs[t - 1], (t - 1) % 2)
            current = following
        products(*pairs[-1], (len(pairs) - 1) % 2)

    table = []
    for g in range(h):
        c = [(s + g) // ob for s in range(ob + 1)]
        first = [g + k * (ob - 1 - 2 * g) for k in c]
        table.append([(f, h + f + s - k * (ob - g)) for s, (k, f) in enumerate(zip(c, first))])
    for g in range(h // 2):
        cols = [(g, ob), (h - 1 - g, h)]
        table.append([(i, h + ob + c) for c, stop in cols for i in range(c, stop)])
    for g in range(h // 2):
        table.append([(c, i - h) for i in (h + g, ob - 1 - g) for c in range(h // 2, i + 1)])

    def pick(kind, entries):
        out = jnp.int32(entries[0])
        for k in range(1, len(entries)):
            if entries[k] != entries[0]:
                out = jnp.where(kind == k, entries[k], out)
        return out

    def open_links():
        pl.semaphore_wait(barrier, quads + 1 + jnp.where(has_slow, 1, 0))

        @pl.when(has_slow)
        def _():
            for copy in halo_out(side_slow, slow):
                copy.start()

        for copy in halo_out(side_fast, fast):
            copy.start()
        for k in range(1, quads):
            for copy in level_copies(k, hi):
                copy.start()
        center_copy.start()

    def take_halo(side):
        first = side * (ob + h)
        for b in range(h):
            fill_j(first + b, xyz_h[side, :, b * bs : (b + 1) * bs], len_h[side, :, b * bs : (b + 1) * bs])
        there = ids_h[side]
        sign = 1 - 2 * side
        base = gid + (2 * side - 1) * ob
        for dj in range(1, HALO + 1):
            wide = jnp.broadcast_to(member(there, base + sign * dj), (ob, bs))
            part_rows = jnp.where(side == 0, wide[h:, :], wide[:h, :])
            for b in range(h):
                mask[mask_at(sign * dj, first + b)] = part_rows[b : b + 1, :]

    def take_fast():
        for copy in halo_arrival(side_fast, fast):
            copy.wait_recv()
        take_halo(side_fast)

    def take_slow():
        @pl.when(has_slow)
        def _():
            for copy in halo_arrival(side_slow, slow):
                copy.wait_recv()

        @pl.when(jnp.logical_not(has_slow))
        def _():
            xyz_h[side_slow] = xyz_ref[:, 0:hb]
            len_h[side_slow] = len_ref[:, 0:hb]
            ids_h[side_slow] = ids_ref[...]
            probes[:, lanes(side_slow * (own + hb), hb)] = probes[:, hb : 2 * hb]

        take_halo(side_slow)

    def level_done():
        for k in range(1, quads):
            for copy in level_copies(k, hi):
                copy.wait()
        for copy in core_copies(core):
            copy.start()

    step_w = min(128, width)

    def partial_sums():
        for copy in core_copies(core):
            copy.wait()
        center_copy.wait()
        centers = cen_all[...].reshape(width, 128).T
        mine = cen_all[slot]
        column = lax.broadcasted_iota(jnp.int32, (ob, width), 1)
        holder = column // ob
        device = holder % quads * 4 + col_y * 2 + holder // quads
        global_ids = (device * ob + column % ob).astype(F32)
        picks = (0, 1, 2, 11)
        pick_r = lax.broadcasted_iota(jnp.int32, (step_w, step_w * half), 0)
        pick_c = lax.broadcasted_iota(jnp.int32, (step_w, step_w * half), 1)
        spread = jnp.where(pick_c // half == pick_r, 1.0, 0.0).astype(BF16)
        eye_r = lax.broadcasted_iota(jnp.int32, (ob * half, step_w * half), 0)
        eye_c = lax.broadcasted_iota(jnp.int32, (ob * half, step_w * half), 1)
        same = lax.rem(eye_r, half) == lax.rem(eye_c, half)
        per = step_w // ob
        totals = []
        for rows in (mine, cen_y[...]):
            coupling = matern([rows[:, c : c + 1] for c in picks], [centers[c : c + 1, :] for c in picks])
            near = jnp.zeros((ob, width), F32)
            for t in range(slots):
                near = jnp.where(rows[:, ROWS + t : ROWS + t + 1] == global_ids, 1.0, near)
            coupling = jnp.where(near > 0.0, 0.0, coupling).astype(BF16)
            total = jnp.zeros((ob * half, 2 * np_), F32)
            for q in range(width // step_w):
                wide = nn(coupling[:, q * step_w : (q + 1) * step_w], spread)
                wide = jnp.concatenate(
                    [jnp.broadcast_to(wide[i : i + 1, :], (half, step_w * half)) for i in range(ob)], axis=0
                )
                kron = jnp.where(same, wide, 0.0).astype(BF16)
                folded = fold_all[q * per : (q + 1) * per].reshape(step_w * half, 2 * np_)
                total = total + nn(kron, folded)
            totals.append(total)
        red_out[...] = totals[1]
        sum_copy.start()
        return totals[0]

    hooks = [(OPEN_AT, open_links), (h, take_fast), (h + h // 2, take_slow)]
    if LEVEL_AT < ob:
        hooks.append((LEVEL_AT, level_done))

    def group(t, carry):
        for at, hook in hooks:
            pl.when(t == at)(hook)
        crossing = t >= h
        kind = jnp.where(crossing, h + (t - h + core * (h // 2)) % h, t)
        sweep(
            [
                (pick(kind, [tiles[s][0] for tiles in table]), pick(kind, [tiles[s][1] for tiles in table]))
                for s in range(ob + 1)
            ]
        )
        g = (kind - h) % (h // 2)
        side = jnp.where(kind < h + h // 2, 1, 0)
        is_fast = t < h + h // 2
        peer = jnp.where(is_fast, fast, slow)

        @pl.when(jnp.logical_and(crossing, jnp.logical_or(is_fast, has_slow)))
        def _():
            part_copy(side, g, peer).start()
            part_copy(side, h - 1 - g, peer).start()

        return carry

    lax.fori_loop(0, ob, group, 0)

    if LEVEL_AT >= ob:
        level_done()
    own_sum = partial_sums()
    loads[5].wait()

    for x in range(h):
        part_arrival(side_fast * h + x, fast).wait_recv()

    @pl.when(has_slow)
    def _():
        for x in range(h):
            part_arrival(side_slow * h + x, slow).wait_recv()

    @pl.when(jnp.logical_not(has_slow))
    def _():
        for x in range(h):
            part[side_slow * h + x] = jnp.zeros((np_, bs), F32)

    sum_copy.wait()
    summed = (own_sum + red_in[...]).astype(BF16)
    for b in range(ob):
        mine = summed[b * half : (b + 1) * half, :]
        far = tn(mine[:, :np_], bout_ref[b, 0:half, :]) + tn(mine[:, np_:], bout_ref[b, half:, :])
        out_ref[:, b * bs : (b + 1) * bs] = acc[h + b] + part[b] + far

    for copy in halo_out(side_fast, fast):
        copy.wait_send()
    for x in range(h):
        part_copy(side_fast, x, fast).wait_send()

    @pl.when(has_slow)
    def _():
        for copy in halo_out(side_slow, slow):
            copy.wait_send()
        for x in range(h):
            part_copy(side_slow, x, slow).wait_send()


def solution(mesh):
    n = mesh.shape["row"]

    def shards(coordinates, length_scale, probes, near_ids, near_count, basis_out, basis_in):
        ob, rank, bs = basis_out.shape
        np_ = probes.shape[0]
        own = ob * bs
        h = ob // 2
        slots = near_ids.shape[1]
        window = ob + 2 * h
        vmem = pl.BlockSpec(memory_space=pltpu.VMEM)
        dma = pltpu.SemaphoreType.DMA
        return pl.pallas_call(
            functools.partial(kernel, n, ob, bs),
            out_shape=jax.ShapeDtypeStruct((np_, own), F32),
            in_specs=[pl.BlockSpec(memory_space=pl.ANY)] * 6,
            out_specs=vmem,
            scratch_shapes=[
                pltpu.VMEM((3, own), F32),
                pltpu.VMEM((1, own), F32),
                pltpu.VMEM((ob, slots), jnp.int32),
                pltpu.VMEM((ob, rank, bs), BF16),
                pltpu.VMEM((ob, rank, bs), BF16),
                pltpu.VMEM((2, 3, h * bs), F32),
                pltpu.VMEM((2, 1, h * bs), F32),
                pltpu.VMEM((2, ob, slots), jnp.int32),
                pltpu.VMEM((np_, window * bs), BF16),
                pltpu.VMEM((ROWS, own), F32),
                pltpu.VMEM((window, ROWS, bs), F32),
                pltpu.VMEM((ob, ROWS, bs), F32),
                pltpu.VMEM((ob, bs, 8 * ROWS), BF16),
                pltpu.VMEM((window, 8 * ROWS, bs), BF16),
                pltpu.VMEM(((2 * HALO + 1) * window + 1, 1, bs), F32),
                pltpu.VMEM((window, np_, bs), F32),
                pltpu.VMEM((ob, np_, bs), F32),
                pltpu.VMEM((n // 2, ob * rank // 2, 2 * np_), BF16),
                pltpu.VMEM((n // 2, ob, 128), F32),
                pltpu.VMEM((ob, 128), F32),
                pltpu.VMEM((ob * rank // 2, 2 * np_), F32),
                pltpu.VMEM((ob * rank // 2, 2 * np_), F32),
                pltpu.VMEM((2, bs, bs), BF16),
                dma((6,)), dma((2, 4)), dma((2, 4)), dma((ob,)), dma((ob,)),
                dma((n // 4,)), dma((n // 4,)), dma((n // 4,)), dma((n // 4,)), dma((4,)), dma((4,)),
            ],
            compiler_params=pltpu.CompilerParams(collective_id=0, has_side_effects=True, vmem_limit_bytes=60 * 1024 * 1024),
        )(coordinates, length_scale.reshape(1, own), probes, near_ids, basis_out, basis_in)

    placed = (
        P(None, ("grp", "row")),
        P(("grp", "row")),
        P(None, ("grp", "row")),
        P(("grp", "row"), None),
        P(("grp", "row")),
        P(("grp", "row"), None, None),
        P(("grp", "row"), None, None),
    )
    return jax.shard_map(
        shards, mesh=mesh, in_specs=placed, out_specs=P(None, ("grp", "row")), check_vma=False
    )
```

time: 30.5 us -> 27.5 us (0.902)
  the two profiles are of different devices: /device:TPU:12 before, /device:TPU:0 now
where the time goes in v2:
time: 27.5 us; the launch traced here: 27.3 us
  Pallas kernels  25.4 us (92%)
  local copies, waits for them, and re-layouts  1.87 us (7%)
    pallas_call x1, Pallas kernels, shards(): pl.pallas_call(functools.partial(kernel, n, ob, bs), out_shape=jax.ShapeD...  25.4 us
    unnamed x1, local copies, waits for them, and re-layouts  1.87 us

profile of v2, /device:TPU:0, one launch (start us, length us, event | category | flops | bytes accessed | tf_op | source)
XLA Modules:
  0.0 27.3 jit_solution(2305665999443788987)
XLA Ops:
  0.0 25.4 %shard_map.64 = f32[64,2048]{1,0:T(8,128)} custom-call(f32[3,2048]{1,0:T(4,128)} %xyz_in.1, f32[1,2048]{1,0:T(1,128)} %bitcast.1, bf16[64,2048]{1,0:T(8,128)(2,1)} %probes_in.1, s32[8,16]{1,0:T(8,128)} %ids_in.1, bf16[8,32,256]{2,1,0:T(8,128)(2,1)} %bout_in.1, bf16[8,32,256]{2,1,0:T(8,128)(2,1)} %bin_in.1), custom_call_target="tpu_custom_call" | custom-call | tf_op jit(solution)/shard_map/pallas_call | solution.py:500
  25.4 1.9 %copy.8 = f32[64,2048]{1,0:T(8,128)} copy(f32[64,2048]{1,0:T(8,128)} %shard_map.64) | data formatting | bytes 1048576
